TPU v7x, 256 devices: a whole 4x4x8 slice. The times are simulated.
256 devices in a mesh: slab: 32 (over x, z), hodlr: 8 (over y, core).
Axes of the slice: x: 4, y: 4, z: 8, core: 2. Of those that a mesh axis runs over, the one named last changes fastest.
Arguments:
- sources: bfloat16 [32, 32, 16384], P('slab', None, 'hodlr'), may hold values from -2 to 2
- leaves: bfloat16 [32, 16, 1024, 1024], P('slab', 'hodlr'), may hold values from -1 to 2
- v_rows: bfloat16 [32, 4, 64, 16384], P('slab', None, None, 'hodlr'), may hold values from -0.0625 to 0.0625
- u_rows: bfloat16 [32, 4, 64, 16384], P('slab', None, None, 'hodlr'), may hold values from -0.1875 to 0.1875
Outputs:
- fronts: bfloat16 [32, 32, 16384], P('slab', None, 'hodlr')
All inputs are finite; a program needn't handle non-finite values.
Results may differ from a plain program's by a relative error of at most 0.025.
Values may be sent and summed in bfloat16 or wider, within the bound.
A program may use at most 64 MiB of HBM per device.

v0:
```python
import jax
import jax.numpy as jnp
from jax import lax
from jax.sharding import PartitionSpec as P


def passed_along(block, axis, distance):
    devices = range(lax.axis_size(axis))
    route = [(i - distance, i) for i in devices if i - distance in devices]
    return lax.ppermute(block, axis, route)


def local(sources, leaves, v_rows, u_rows):
    devices = lax.axis_size("hodlr")
    chain = lax.axis_size("slab")
    position = lax.axis_index("slab")
    member = lax.axis_index("hodlr")
    cross = devices.bit_length() - 1
    source = sources[0]
    leaf = leaves[0]
    right = v_rows[0]
    left = u_rows[0]
    shot_batch, width = source.shape
    rank = right.shape[1]
    nleaf = leaf.shape[0]
    leaf_size = leaf.shape[1]
    peers = jnp.arange(devices, dtype=jnp.int32)
    sibling_rows = []
    for tree_level in range(1, cross + 1):
        group = devices >> tree_level
        sibling_rows.append(
            (peers // group == jnp.bitwise_xor(member // group, 1)).astype(jnp.float32)
        )
    sibling_mask = jnp.stack(sibling_rows)

    def partials_of(w, factors):
        rows = w.shape[0]
        return jnp.einsum("sn,crn->csr", w, factors, preferred_element_type=jnp.float32).reshape(
            cross, rows * rank
        )

    def combine_gathered(gathered, rows):
        sibling = jnp.einsum("pcx,cp->cx", gathered, sibling_mask, precision=lax.Precision.HIGHEST)
        return sibling.reshape(cross, rows, rank).astype(jnp.bfloat16)

    def local_part(w):
        rows = w.shape[0]
        sweep_output = jnp.einsum(
            "sbj,bjo->sbo",
            w.reshape(rows, nleaf, leaf_size),
            leaf,
            preferred_element_type=jnp.float32,
        ).reshape(rows, width)
        block_size = width * devices >> 4
        block_list = width // block_size
        projection_rows = jnp.einsum(
            "kqc,vqc->kqv",
            w.reshape(rows, block_list, block_size),
            right[3].reshape(rank, block_list, block_size),
            preferred_element_type=jnp.float32,
        ).astype(jnp.bfloat16)
        swapped_halves = projection_rows.reshape(rows, block_list // 2, 2, rank)[
            :, :, ::-1
        ].reshape(rows, block_list, rank)
        sweep_output = sweep_output + jnp.einsum(
            "cwp,pwi->cwi",
            swapped_halves,
            left[3].reshape(rank, block_list, block_size),
            preferred_element_type=jnp.float32,
        ).reshape(rows, width)
        return sweep_output

    def finish(sweep_output, sibling):
        sweep_output = sweep_output + jnp.einsum(
            "csr,crn->sn", sibling, left[:cross], preferred_element_type=jnp.float32
        )
        return sweep_output.astype(jnp.bfloat16)

    def apply(w):
        rows = w.shape[0]
        partial_value = partials_of(w, right[:cross])
        sweep_output = local_part(w)
        gathered = lax.all_gather(partial_value[None], "hodlr", axis=0, tiled=True)
        sibling = combine_gathered(gathered, rows)
        return finish(sweep_output, sibling)

    groups = 1
    batch = shot_batch // groups

    def advance(step, carry):
        front, swept = carry
        incoming = passed_along(front, "slab", 1)
        offset = step - position
        valid = (offset >= 0) & (offset < groups)
        w = (source.astype(jnp.float32) + incoming.astype(jnp.float32)).astype(jnp.bfloat16)
        sweep_output = apply(w)
        current = swept
        swept = jnp.where(valid, sweep_output, current)
        return (sweep_output, swept)

    initial = (
        jnp.zeros((batch, width), jnp.bfloat16),
        jnp.zeros((shot_batch, width), jnp.bfloat16),
    )
    _, swept = lax.fori_loop(0, chain + groups - 1, advance, initial)
    return swept[None]


def solution(mesh):
    in_specs = (
        P("slab", None, "hodlr"),
        P("slab", "hodlr", None, None),
        P("slab", None, None, "hodlr"),
        P("slab", None, None, "hodlr"),
    )
    out_specs = P("slab", None, "hodlr")
    return jax.shard_map(local, mesh=mesh, in_specs=in_specs, out_specs=out_specs, check_vma=False)
```

profile of v0, /device:TPU:7, one launch (start us, length us, event | category | flops | bytes accessed | tf_op | source)
XLA Modules:
  0.0 952.1 jit_solution(5715799266085852439)
XLA Ops:
  0.1 951.3 %while.16 = (s32[]{:T(128)}, bf16[32,2048]{1,0:T(8,128)(2,1)S(1)}, bf16[32,2048]{1,0:T(8,128)(2,1)S(1)}, bf16[32,2048]{1,0:T(8,128)(2,1)}, bf16[2,1024,1024]{2,1...) while((s32[]{:T(128)}, bf16[32,2048]{1,0:T(8,128)(2,1)S(1)}, ...), condition=%wide.region_1.2_spmd.clone, body=%wide.region_0.1_spmd.clone.sunk | while | flops 202575872 | bytes 16732478 | solution.py:105
  6.0 5.1 collective-permute-done
  17.2 14.4 %all_gather.9 = f32[8,3,2048]{2,1,0:T(4,128)S(1)} all-gather(f32[1,3,2048]{2,1,0:T(4,128)S(1)} %reshape.133), channel_id=1, replica_groups=mesh['slab'=32,'hodlr'=8] {'hodlr'}, dimensions={0}, use_global_device_ids=true | all-gather | bytes 221184 | tf_op jit(solution)/shard_map/while/body/eval_jaxpr/all_gather | solution.py:83
  36.8 4.6 collective-permute-done
  47.6 13.7 %all_gather.9 = f32[8,3,2048]{2,1,0:T(4,128)S(1)} all-gather(f32[1,3,2048]{2,1,0:T(4,128)S(1)} %reshape.133), channel_id=1, replica_groups=mesh['slab'=32,'hodlr'=8] {'hodlr'}, dimensions={0}, use_global_device_ids=true | all-gather | bytes 221184 | tf_op jit(solution)/shard_map/while/body/eval_jaxpr/all_gather | solution.py:83
  66.4 4.6 collective-permute-done
  77.2 13.7 %all_gather.9 = f32[8,3,2048]{2,1,0:T(4,128)S(1)} all-gather(f32[1,3,2048]{2,1,0:T(4,128)S(1)} %reshape.133), channel_id=1, replica_groups=mesh['slab'=32,'hodlr'=8] {'hodlr'}, dimensions={0}, use_global_device_ids=true | all-gather | bytes 221184 | tf_op jit(solution)/shard_map/while/body/eval_jaxpr/all_gather | solution.py:83
  96.1 4.6 collective-permute-done
  106.9 13.7 %all_gather.9 = f32[8,3,2048]{2,1,0:T(4,128)S(1)} all-gather(f32[1,3,2048]{2,1,0:T(4,128)S(1)} %reshape.133), channel_id=1, replica_groups=mesh['slab'=32,'hodlr'=8] {'hodlr'}, dimensions={0}, use_global_device_ids=true | all-gather | bytes 221184 | tf_op jit(solution)/shard_map/while/body/eval_jaxpr/all_gather | solution.py:83
  125.7 4.6 collective-permute-done
  136.5 13.7 %all_gather.9 = f32[8,3,2048]{2,1,0:T(4,128)S(1)} all-gather(f32[1,3,2048]{2,1,0:T(4,128)S(1)} %reshape.133), channel_id=1, replica_groups=mesh['slab'=32,'hodlr'=8] {'hodlr'}, dimensions={0}, use_global_device_ids=true | all-gather | bytes 221184 | tf_op jit(solution)/shard_map/while/body/eval_jaxpr/all_gather | solution.py:83
  155.4 4.6 collective-permute-done
  166.2 13.7 %all_gather.9 = f32[8,3,2048]{2,1,0:T(4,128)S(1)} all-gather(f32[1,3,2048]{2,1,0:T(4,128)S(1)} %reshape.133), channel_id=1, replica_groups=mesh['slab'=32,'hodlr'=8] {'hodlr'}, dimensions={0}, use_global_device_ids=true | all-gather | bytes 221184 | tf_op jit(solution)/shard_map/while/body/eval_jaxpr/all_gather | solution.py:83
  185.0 4.6 collective-permute-done
  195.8 13.7 %all_gather.9 = f32[8,3,2048]{2,1,0:T(4,128)S(1)} all-gather(f32[1,3,2048]{2,1,0:T(4,128)S(1)} %reshape.133), channel_id=1, replica_groups=mesh['slab'=32,'hodlr'=8] {'hodlr'}, dimensions={0}, use_global_device_ids=true | all-gather | bytes 221184 | tf_op jit(solution)/shard_map/while/body/eval_jaxpr/all_gather | solution.py:83
  214.7 4.6 collective-permute-done
  225.4 13.7 %all_gather.9 = f32[8,3,2048]{2,1,0:T(4,128)S(1)} all-gather(f32[1,3,2048]{2,1,0:T(4,128)S(1)} %reshape.133), channel_id=1, replica_groups=mesh['slab'=32,'hodlr'=8] {'hodlr'}, dimensions={0}, use_global_device_ids=true | all-gather | bytes 221184 | tf_op jit(solution)/shard_map/while/body/eval_jaxpr/all_gather | solution.py:83
  244.3 4.6 collective-permute-done
  255.1 13.7 %all_gather.9 = f32[8,3,2048]{2,1,0:T(4,128)S(1)} all-gather(f32[1,3,2048]{2,1,0:T(4,128)S(1)} %reshape.133), channel_id=1, replica_groups=mesh['slab'=32,'hodlr'=8] {'hodlr'}, dimensions={0}, use_global_device_ids=true | all-gather | bytes 221184 | tf_op jit(solution)/shard_map/while/body/eval_jaxpr/all_gather | solution.py:83
  273.9 4.6 collective-permute-done
  284.7 13.7 %all_gather.9 = f32[8,3,2048]{2,1,0:T(4,128)S(1)} all-gather(f32[1,3,2048]{2,1,0:T(4,128)S(1)} %reshape.133), channel_id=1, replica_groups=mesh['slab'=32,'hodlr'=8] {'hodlr'}, dimensions={0}, use_global_device_ids=true | all-gather | bytes 221184 | tf_op jit(solution)/shard_map/while/body/eval_jaxpr/all_gather | solution.py:83
  303.6 4.6 collective-permute-done
  314.4 13.7 %all_gather.9 = f32[8,3,2048]{2,1,0:T(4,128)S(1)} all-gather(f32[1,3,2048]{2,1,0:T(4,128)S(1)} %reshape.133), channel_id=1, replica_groups=mesh['slab'=32,'hodlr'=8] {'hodlr'}, dimensions={0}, use_global_device_ids=true | all-gather | bytes 221184 | tf_op jit(solution)/shard_map/while/body/eval_jaxpr/all_gather | solution.py:83
  333.2 4.6 collective-permute-done
  344.0 13.7 %all_gather.9 = f32[8,3,2048]{2,1,0:T(4,128)S(1)} all-gather(f32[1,3,2048]{2,1,0:T(4,128)S(1)} %reshape.133), channel_id=1, replica_groups=mesh['slab'=32,'hodlr'=8] {'hodlr'}, dimensions={0}, use_global_device_ids=true | all-gather | bytes 221184 | tf_op jit(solution)/shard_map/while/body/eval_jaxpr/all_gather | solution.py:83
  362.9 4.6 collective-permute-done
  373.7 13.7 %all_gather.9 = f32[8,3,2048]{2,1,0:T(4,128)S(1)} all-gather(f32[1,3,2048]{2,1,0:T(4,128)S(1)} %reshape.133), channel_id=1, replica_groups=mesh['slab'=32,'hodlr'=8] {'hodlr'}, dimensions={0}, use_global_device_ids=true | all-gather | bytes 221184 | tf_op jit(solution)/shard_map/while/body/eval_jaxpr/all_gather | solution.py:83
  392.5 4.6 collective-permute-done
  403.3 13.7 %all_gather.9 = f32[8,3,2048]{2,1,0:T(4,128)S(1)} all-gather(f32[1,3,2048]{2,1,0:T(4,128)S(1)} %reshape.133), channel_id=1, replica_groups=mesh['slab'=32,'hodlr'=8] {'hodlr'}, dimensions={0}, use_global_device_ids=true | all-gather | bytes 221184 | tf_op jit(solution)/shard_map/while/body/eval_jaxpr/all_gather | solution.py:83
  422.2 4.6 collective-permute-done
  432.9 13.7 %all_gather.9 = f32[8,3,2048]{2,1,0:T(4,128)S(1)} all-gather(f32[1,3,2048]{2,1,0:T(4,128)S(1)} %reshape.133), channel_id=1, replica_groups=mesh['slab'=32,'hodlr'=8] {'hodlr'}, dimensions={0}, use_global_device_ids=true | all-gather | bytes 221184 | tf_op jit(solution)/shard_map/while/body/eval_jaxpr/all_gather | solution.py:83
  451.8 4.6 collective-permute-done
  462.6 13.7 %all_gather.9 = f32[8,3,2048]{2,1,0:T(4,128)S(1)} all-gather(f32[1,3,2048]{2,1,0:T(4,128)S(1)} %reshape.133), channel_id=1, replica_groups=mesh['slab'=32,'hodlr'=8] {'hodlr'}, dimensions={0}, use_global_device_ids=true | all-gather | bytes 221184 | tf_op jit(solution)/shard_map/while/body/eval_jaxpr/all_gather | solution.py:83
  481.4 4.6 collective-permute-done
  492.2 13.7 %all_gather.9 = f32[8,3,2048]{2,1,0:T(4,128)S(1)} all-gather(f32[1,3,2048]{2,1,0:T(4,128)S(1)} %reshape.133), channel_id=1, replica_groups=mesh['slab'=32,'hodlr'=8] {'hodlr'}, dimensions={0}, use_global_device_ids=true | all-gather | bytes 221184 | tf_op jit(solution)/shard_map/while/body/eval_jaxpr/all_gather | solution.py:83
  511.1 4.6 collective-permute-done
  521.9 13.7 %all_gather.9 = f32[8,3,2048]{2,1,0:T(4,128)S(1)} all-gather(f32[1,3,2048]{2,1,0:T(4,128)S(1)} %reshape.133), channel_id=1, replica_groups=mesh['slab'=32,'hodlr'=8] {'hodlr'}, dimensions={0}, use_global_device_ids=true | all-gather | bytes 221184 | tf_op jit(solution)/shard_map/while/body/eval_jaxpr/all_gather | solution.py:83
  540.7 4.6 collective-permute-done
  551.5 13.7 %all_gather.9 = f32[8,3,2048]{2,1,0:T(4,128)S(1)} all-gather(f32[1,3,2048]{2,1,0:T(4,128)S(1)} %reshape.133), channel_id=1, replica_groups=mesh['slab'=32,'hodlr'=8] {'hodlr'}, dimensions={0}, use_global_device_ids=true | all-gather | bytes 221184 | tf_op jit(solution)/shard_map/while/body/eval_jaxpr/all_gather | solution.py:83
  570.4 4.6 collective-permute-done
  581.1 13.7 %all_gather.9 = f32[8,3,2048]{2,1,0:T(4,128)S(1)} all-gather(f32[1,3,2048]{2,1,0:T(4,128)S(1)} %reshape.133), channel_id=1, replica_groups=mesh['slab'=32,'hodlr'=8] {'hodlr'}, dimensions={0}, use_global_device_ids=true | all-gather | bytes 221184 | tf_op jit(solution)/shard_map/while/body/eval_jaxpr/all_gather | solution.py:83
  600.0 4.6 collective-permute-done
  610.8 13.7 %all_gather.9 = f32[8,3,2048]{2,1,0:T(4,128)S(1)} all-gather(f32[1,3,2048]{2,1,0:T(4,128)S(1)} %reshape.133), channel_id=1, replica_groups=mesh['slab'=32,'hodlr'=8] {'hodlr'}, dimensions={0}, use_global_device_ids=true | all-gather | bytes 221184 | tf_op jit(solution)/shard_map/while/body/eval_jaxpr/all_gather | solution.py:83
  629.6 4.6 collective-permute-done
  640.4 13.7 %all_gather.9 = f32[8,3,2048]{2,1,0:T(4,128)S(1)} all-gather(f32[1,3,2048]{2,1,0:T(4,128)S(1)} %reshape.133), channel_id=1, replica_groups=mesh['slab'=32,'hodlr'=8] {'hodlr'}, dimensions={0}, use_global_device_ids=true | all-gather | bytes 221184 | tf_op jit(solution)/shard_map/while/body/eval_jaxpr/all_gather | solution.py:83
  659.3 4.6 collective-permute-done
  670.1 13.7 %all_gather.9 = f32[8,3,2048]{2,1,0:T(4,128)S(1)} all-gather(f32[1,3,2048]{2,1,0:T(4,128)S(1)} %reshape.133), channel_id=1, replica_groups=mesh['slab'=32,'hodlr'=8] {'hodlr'}, dimensions={0}, use_global_device_ids=true | all-gather | bytes 221184 | tf_op jit(solution)/shard_map/while/body/eval_jaxpr/all_gather | solution.py:83
  688.9 4.6 collective-permute-done
  699.7 13.7 %all_gather.9 = f32[8,3,2048]{2,1,0:T(4,128)S(1)} all-gather(f32[1,3,2048]{2,1,0:T(4,128)S(1)} %reshape.133), channel_id=1, replica_groups=mesh['slab'=32,'hodlr'=8] {'hodlr'}, dimensions={0}, use_global_device_ids=true | all-gather | bytes 221184 | tf_op jit(solution)/shard_map/while/body/eval_jaxpr/all_gather | solution.py:83
  718.6 4.6 collective-permute-done
  729.4 13.7 %all_gather.9 = f32[8,3,2048]{2,1,0:T(4,128)S(1)} all-gather(f32[1,3,2048]{2,1,0:T(4,128)S(1)} %reshape.133), channel_id=1, replica_groups=mesh['slab'=32,'hodlr'=8] {'hodlr'}, dimensions={0}, use_global_device_ids=true | all-gather | bytes 221184 | tf_op jit(solution)/shard_map/while/body/eval_jaxpr/all_gather | solution.py:83
  748.2 4.6 collective-permute-done
  759.0 13.7 %all_gather.9 = f32[8,3,2048]{2,1,0:T(4,128)S(1)} all-gather(f32[1,3,2048]{2,1,0:T(4,128)S(1)} %reshape.133), channel_id=1, replica_groups=mesh['slab'=32,'hodlr'=8] {'hodlr'}, dimensions={0}, use_global_device_ids=true | all-gather | bytes 221184 | tf_op jit(solution)/shard_map/while/body/eval_jaxpr/all_gather | solution.py:83
  777.9 4.6 collective-permute-done
  788.6 13.7 %all_gather.9 = f32[8,3,2048]{2,1,0:T(4,128)S(1)} all-gather(f32[1,3,2048]{2,1,0:T(4,128)S(1)} %reshape.133), channel_id=1, replica_groups=mesh['slab'=32,'hodlr'=8] {'hodlr'}, dimensions={0}, use_global_device_ids=true | all-gather | bytes 221184 | tf_op jit(solution)/shard_map/while/body/eval_jaxpr/all_gather | solution.py:83
  807.5 4.6 collective-permute-done
  818.3 13.7 %all_gather.9 = f32[8,3,2048]{2,1,0:T(4,128)S(1)} all-gather(f32[1,3,2048]{2,1,0:T(4,128)S(1)} %reshape.133), channel_id=1, replica_groups=mesh['slab'=32,'hodlr'=8] {'hodlr'}, dimensions={0}, use_global_device_ids=true | all-gather | bytes 221184 | tf_op jit(solution)/shard_map/while/body/eval_jaxpr/all_gather | solution.py:83
  837.1 4.6 collective-permute-done
  847.9 13.7 %all_gather.9 = f32[8,3,2048]{2,1,0:T(4,128)S(1)} all-gather(f32[1,3,2048]{2,1,0:T(4,128)S(1)} %reshape.133), channel_id=1, replica_groups=mesh['slab'=32,'hodlr'=8] {'hodlr'}, dimensions={0}, use_global_device_ids=true | all-gather | bytes 221184 | tf_op jit(solution)/shard_map/while/body/eval_jaxpr/all_gather | solution.py:83
  866.8 4.6 collective-permute-done
  877.6 13.7 %all_gather.9 = f32[8,3,2048]{2,1,0:T(4,128)S(1)} all-gather(f32[1,3,2048]{2,1,0:T(4,128)S(1)} %reshape.133), channel_id=1, replica_groups=mesh['slab'=32,'hodlr'=8] {'hodlr'}, dimensions={0}, use_global_device_ids=true | all-gather | bytes 221184 | tf_op jit(solution)/shard_map/while/body/eval_jaxpr/all_gather | solution.py:83
  907.2 13.7 %all_gather.9 = f32[8,3,2048]{2,1,0:T(4,128)S(1)} all-gather(f32[1,3,2048]{2,1,0:T(4,128)S(1)} %reshape.133), channel_id=1, replica_groups=mesh['slab'=32,'hodlr'=8] {'hodlr'}, dimensions={0}, use_global_device_ids=true | all-gather | bytes 221184 | tf_op jit(solution)/shard_map/while/body/eval_jaxpr/all_gather | solution.py:83
  926.1 4.6 collective-permute-done
  936.9 13.7 %all_gather.9 = f32[8,3,2048]{2,1,0:T(4,128)S(1)} all-gather(f32[1,3,2048]{2,1,0:T(4,128)S(1)} %reshape.133), channel_id=1, replica_groups=mesh['slab'=32,'hodlr'=8] {'hodlr'}, dimensions={0}, use_global_device_ids=true | all-gather | bytes 221184 | tf_op jit(solution)/shard_map/while/body/eval_jaxpr/all_gather | solution.py:83
  (648 shorter events, 365.1 us)
Async XLA Ops:
  0.1 10.9 %collective-permute-start = (bf16[32,2048]{1,0:T(8,128)(2,1)S(1)}, bf16[32,2048]{1,0:T(8,128)(2,1)S(1)}, u32[]{:S(2)}, u32[]{:S(2)}) collective-permute-start(bf16[32,2048]{1,0:T(8,128)(2,1)S(1)} %broadcast_select_fusion.2), channel_id=1, source_target_pairs={{0,8},{8,16},{16,24},{24,32},{32,40},{40,48},{48,56},{56,64},{64,7... | collective-permute-start | bytes 393224 | tf_op jit(solution)/shard_map/while/body/eval_jaxpr/ppermute | solution.py:10
  12.0 20.2 %copy-start = (bf16[4,64,2048]{2,1,0:T(8,128)(2,1)S(1)}, bf16[4,64,2048]{2,1,0:T(8,128)(2,1)}, u32[]{:S(2)}) copy-start(bf16[4,64,2048]{2,1,0:T(8,128)(2,1)} %get-tuple-element.299) | copy-start | bytes 3145732 | tf_op jit(solution)/shard_map/while
  32.5 8.9 collective-permute-start
  42.4 19.5 %copy-start = (bf16[4,64,2048]{2,1,0:T(8,128)(2,1)S(1)}, bf16[4,64,2048]{2,1,0:T(8,128)(2,1)}, u32[]{:S(2)}) copy-start(bf16[4,64,2048]{2,1,0:T(8,128)(2,1)} %get-tuple-element.299) | copy-start | bytes 3145732 | tf_op jit(solution)/shard_map/while
  62.2 8.9 collective-permute-start
  72.0 19.5 %copy-start = (bf16[4,64,2048]{2,1,0:T(8,128)(2,1)S(1)}, bf16[4,64,2048]{2,1,0:T(8,128)(2,1)}, u32[]{:S(2)}) copy-start(bf16[4,64,2048]{2,1,0:T(8,128)(2,1)} %get-tuple-element.299) | copy-start | bytes 3145732 | tf_op jit(solution)/shard_map/while
  91.8 8.9 collective-permute-start
  101.7 19.5 %copy-start = (bf16[4,64,2048]{2,1,0:T(8,128)(2,1)S(1)}, bf16[4,64,2048]{2,1,0:T(8,128)(2,1)}, u32[]{:S(2)}) copy-start(bf16[4,64,2048]{2,1,0:T(8,128)(2,1)} %get-tuple-element.299) | copy-start | bytes 3145732 | tf_op jit(solution)/shard_map/while
  121.5 8.9 collective-permute-start
  131.3 19.5 %copy-start = (bf16[4,64,2048]{2,1,0:T(8,128)(2,1)S(1)}, bf16[4,64,2048]{2,1,0:T(8,128)(2,1)}, u32[]{:S(2)}) copy-start(bf16[4,64,2048]{2,1,0:T(8,128)(2,1)} %get-tuple-element.299) | copy-start | bytes 3145732 | tf_op jit(solution)/shard_map/while
  151.1 8.9 collective-permute-start
  160.9 19.5 %copy-start = (bf16[4,64,2048]{2,1,0:T(8,128)(2,1)S(1)}, bf16[4,64,2048]{2,1,0:T(8,128)(2,1)}, u32[]{:S(2)}) copy-start(bf16[4,64,2048]{2,1,0:T(8,128)(2,1)} %get-tuple-element.299) | copy-start | bytes 3145732 | tf_op jit(solution)/shard_map/while
  180.8 8.9 collective-permute-start
  190.6 19.5 %copy-start = (bf16[4,64,2048]{2,1,0:T(8,128)(2,1)S(1)}, bf16[4,64,2048]{2,1,0:T(8,128)(2,1)}, u32[]{:S(2)}) copy-start(bf16[4,64,2048]{2,1,0:T(8,128)(2,1)} %get-tuple-element.299) | copy-start | bytes 3145732 | tf_op jit(solution)/shard_map/while
  210.4 8.9 collective-permute-start
  220.2 19.5 %copy-start = (bf16[4,64,2048]{2,1,0:T(8,128)(2,1)S(1)}, bf16[4,64,2048]{2,1,0:T(8,128)(2,1)}, u32[]{:S(2)}) copy-start(bf16[4,64,2048]{2,1,0:T(8,128)(2,1)} %get-tuple-element.299) | copy-start | bytes 3145732 | tf_op jit(solution)/shard_map/while
  240.0 8.9 collective-permute-start
  249.9 19.5 %copy-start = (bf16[4,64,2048]{2,1,0:T(8,128)(2,1)S(1)}, bf16[4,64,2048]{2,1,0:T(8,128)(2,1)}, u32[]{:S(2)}) copy-start(bf16[4,64,2048]{2,1,0:T(8,128)(2,1)} %get-tuple-element.299) | copy-start | bytes 3145732 | tf_op jit(solution)/shard_map/while
  269.7 8.9 collective-permute-start
  279.5 19.5 %copy-start = (bf16[4,64,2048]{2,1,0:T(8,128)(2,1)S(1)}, bf16[4,64,2048]{2,1,0:T(8,128)(2,1)}, u32[]{:S(2)}) copy-start(bf16[4,64,2048]{2,1,0:T(8,128)(2,1)} %get-tuple-element.299) | copy-start | bytes 3145732 | tf_op jit(solution)/shard_map/while
  299.3 8.9 collective-permute-start
  309.2 19.5 %copy-start = (bf16[4,64,2048]{2,1,0:T(8,128)(2,1)S(1)}, bf16[4,64,2048]{2,1,0:T(8,128)(2,1)}, u32[]{:S(2)}) copy-start(bf16[4,64,2048]{2,1,0:T(8,128)(2,1)} %get-tuple-element.299) | copy-start | bytes 3145732 | tf_op jit(solution)/shard_map/while
  329.0 8.9 collective-permute-start
  338.8 19.5 %copy-start = (bf16[4,64,2048]{2,1,0:T(8,128)(2,1)S(1)}, bf16[4,64,2048]{2,1,0:T(8,128)(2,1)}, u32[]{:S(2)}) copy-start(bf16[4,64,2048]{2,1,0:T(8,128)(2,1)} %get-tuple-element.299) | copy-start | bytes 3145732 | tf_op jit(solution)/shard_map/while
  358.6 8.9 collective-permute-start
  368.4 19.5 %copy-start = (bf16[4,64,2048]{2,1,0:T(8,128)(2,1)S(1)}, bf16[4,64,2048]{2,1,0:T(8,128)(2,1)}, u32[]{:S(2)}) copy-start(bf16[4,64,2048]{2,1,0:T(8,128)(2,1)} %get-tuple-element.299) | copy-start | bytes 3145732 | tf_op jit(solution)/shard_map/while
  388.3 8.9 collective-permute-start
  398.1 19.5 %copy-start = (bf16[4,64,2048]{2,1,0:T(8,128)(2,1)S(1)}, bf16[4,64,2048]{2,1,0:T(8,128)(2,1)}, u32[]{:S(2)}) copy-start(bf16[4,64,2048]{2,1,0:T(8,128)(2,1)} %get-tuple-element.299) | copy-start | bytes 3145732 | tf_op jit(solution)/shard_map/while
  417.9 8.9 collective-permute-start
  427.7 19.5 %copy-start = (bf16[4,64,2048]{2,1,0:T(8,128)(2,1)S(1)}, bf16[4,64,2048]{2,1,0:T(8,128)(2,1)}, u32[]{:S(2)}) copy-start(bf16[4,64,2048]{2,1,0:T(8,128)(2,1)} %get-tuple-element.299) | copy-start | bytes 3145732 | tf_op jit(solution)/shard_map/while
  447.5 8.9 collective-permute-start
  457.4 19.5 %copy-start = (bf16[4,64,2048]{2,1,0:T(8,128)(2,1)S(1)}, bf16[4,64,2048]{2,1,0:T(8,128)(2,1)}, u32[]{:S(2)}) copy-start(bf16[4,64,2048]{2,1,0:T(8,128)(2,1)} %get-tuple-element.299) | copy-start | bytes 3145732 | tf_op jit(solution)/shard_map/while
  477.2 8.9 collective-permute-start
  487.0 19.5 %copy-start = (bf16[4,64,2048]{2,1,0:T(8,128)(2,1)S(1)}, bf16[4,64,2048]{2,1,0:T(8,128)(2,1)}, u32[]{:S(2)}) copy-start(bf16[4,64,2048]{2,1,0:T(8,128)(2,1)} %get-tuple-element.299) | copy-start | bytes 3145732 | tf_op jit(solution)/shard_map/while
  506.8 8.9 collective-permute-start
  516.6 19.5 %copy-start = (bf16[4,64,2048]{2,1,0:T(8,128)(2,1)S(1)}, bf16[4,64,2048]{2,1,0:T(8,128)(2,1)}, u32[]{:S(2)}) copy-start(bf16[4,64,2048]{2,1,0:T(8,128)(2,1)} %get-tuple-element.299) | copy-start | bytes 3145732 | tf_op jit(solution)/shard_map/while
  536.5 8.9 collective-permute-start
  546.3 19.5 %copy-start = (bf16[4,64,2048]{2,1,0:T(8,128)(2,1)S(1)}, bf16[4,64,2048]{2,1,0:T(8,128)(2,1)}, u32[]{:S(2)}) copy-start(bf16[4,64,2048]{2,1,0:T(8,128)(2,1)} %get-tuple-element.299) | copy-start | bytes 3145732 | tf_op jit(solution)/shard_map/while
  566.1 8.9 collective-permute-start
  575.9 19.5 %copy-start = (bf16[4,64,2048]{2,1,0:T(8,128)(2,1)S(1)}, bf16[4,64,2048]{2,1,0:T(8,128)(2,1)}, u32[]{:S(2)}) copy-start(bf16[4,64,2048]{2,1,0:T(8,128)(2,1)} %get-tuple-element.299) | copy-start | bytes 3145732 | tf_op jit(solution)/shard_map/while
  595.7 8.9 collective-permute-start
  605.6 19.5 %copy-start = (bf16[4,64,2048]{2,1,0:T(8,128)(2,1)S(1)}, bf16[4,64,2048]{2,1,0:T(8,128)(2,1)}, u32[]{:S(2)}) copy-start(bf16[4,64,2048]{2,1,0:T(8,128)(2,1)} %get-tuple-element.299) | copy-start | bytes 3145732 | tf_op jit(solution)/shard_map/while
  625.4 8.9 collective-permute-start
  635.2 19.5 %copy-start = (bf16[4,64,2048]{2,1,0:T(8,128)(2,1)S(1)}, bf16[4,64,2048]{2,1,0:T(8,128)(2,1)}, u32[]{:S(2)}) copy-start(bf16[4,64,2048]{2,1,0:T(8,128)(2,1)} %get-tuple-element.299) | copy-start | bytes 3145732 | tf_op jit(solution)/shard_map/while
  655.0 8.9 collective-permute-start
  664.9 19.5 %copy-start = (bf16[4,64,2048]{2,1,0:T(8,128)(2,1)S(1)}, bf16[4,64,2048]{2,1,0:T(8,128)(2,1)}, u32[]{:S(2)}) copy-start(bf16[4,64,2048]{2,1,0:T(8,128)(2,1)} %get-tuple-element.299) | copy-start | bytes 3145732 | tf_op jit(solution)/shard_map/while
  684.7 8.9 collective-permute-start
  694.5 19.5 %copy-start = (bf16[4,64,2048]{2,1,0:T(8,128)(2,1)S(1)}, bf16[4,64,2048]{2,1,0:T(8,128)(2,1)}, u32[]{:S(2)}) copy-start(bf16[4,64,2048]{2,1,0:T(8,128)(2,1)} %get-tuple-element.299) | copy-start | bytes 3145732 | tf_op jit(solution)/shard_map/while
  714.3 8.9 collective-permute-start
  724.1 19.5 %copy-start = (bf16[4,64,2048]{2,1,0:T(8,128)(2,1)S(1)}, bf16[4,64,2048]{2,1,0:T(8,128)(2,1)}, u32[]{:S(2)}) copy-start(bf16[4,64,2048]{2,1,0:T(8,128)(2,1)} %get-tuple-element.299) | copy-start | bytes 3145732 | tf_op jit(solution)/shard_map/while
  744.0 8.9 collective-permute-start
  753.8 19.5 %copy-start = (bf16[4,64,2048]{2,1,0:T(8,128)(2,1)S(1)}, bf16[4,64,2048]{2,1,0:T(8,128)(2,1)}, u32[]{:S(2)}) copy-start(bf16[4,64,2048]{2,1,0:T(8,128)(2,1)} %get-tuple-element.299) | copy-start | bytes 3145732 | tf_op jit(solution)/shard_map/while
  773.6 8.9 collective-permute-start
  783.4 19.5 %copy-start = (bf16[4,64,2048]{2,1,0:T(8,128)(2,1)S(1)}, bf16[4,64,2048]{2,1,0:T(8,128)(2,1)}, u32[]{:S(2)}) copy-start(bf16[4,64,2048]{2,1,0:T(8,128)(2,1)} %get-tuple-element.299) | copy-start | bytes 3145732 | tf_op jit(solution)/shard_map/while
  803.2 8.9 collective-permute-start
  813.1 19.5 %copy-start = (bf16[4,64,2048]{2,1,0:T(8,128)(2,1)S(1)}, bf16[4,64,2048]{2,1,0:T(8,128)(2,1)}, u32[]{:S(2)}) copy-start(bf16[4,64,2048]{2,1,0:T(8,128)(2,1)} %get-tuple-element.299) | copy-start | bytes 3145732 | tf_op jit(solution)/shard_map/while
  832.9 8.9 collective-permute-start
  842.7 19.5 %copy-start = (bf16[4,64,2048]{2,1,0:T(8,128)(2,1)S(1)}, bf16[4,64,2048]{2,1,0:T(8,128)(2,1)}, u32[]{:S(2)}) copy-start(bf16[4,64,2048]{2,1,0:T(8,128)(2,1)} %get-tuple-element.299) | copy-start | bytes 3145732 | tf_op jit(solution)/shard_map/while
  862.5 8.9 collective-permute-start
  872.4 19.5 %copy-start = (bf16[4,64,2048]{2,1,0:T(8,128)(2,1)S(1)}, bf16[4,64,2048]{2,1,0:T(8,128)(2,1)}, u32[]{:S(2)}) copy-start(bf16[4,64,2048]{2,1,0:T(8,128)(2,1)} %get-tuple-element.299) | copy-start | bytes 3145732 | tf_op jit(solution)/shard_map/while
  892.2 8.9 collective-permute-start
  902.0 19.5 %copy-start = (bf16[4,64,2048]{2,1,0:T(8,128)(2,1)S(1)}, bf16[4,64,2048]{2,1,0:T(8,128)(2,1)}, u32[]{:S(2)}) copy-start(bf16[4,64,2048]{2,1,0:T(8,128)(2,1)} %get-tuple-element.299) | copy-start | bytes 3145732 | tf_op jit(solution)/shard_map/while
  921.8 8.9 collective-permute-start
  931.6 19.5 %copy-start = (bf16[4,64,2048]{2,1,0:T(8,128)(2,1)S(1)}, bf16[4,64,2048]{2,1,0:T(8,128)(2,1)}, u32[]{:S(2)}) copy-start(bf16[4,64,2048]{2,1,0:T(8,128)(2,1)} %get-tuple-element.299) | copy-start | bytes 3145732 | tf_op jit(solution)/shard_map/while
  (1 other events, 0.7 us)
where the time goes:
time: 958 us; the launch traced here: 952 us
  blocking collectives  439 us (46%)
  matrix products  185 us (19%)
  waiting for transfers between devices  149 us (16%)
  local copies, waits for them, and re-layouts  81.8 us (9%)
  starting transfers between devices  63.1 us (7%)
  other arithmetic  30.5 us (3%)
    all_gather x32, blocking collectives, apply(): gathered = lax.all_gather(partial_value[None], 'hodlr', axis=0, tiled=True)  439 us
    ppermute x32, waiting for transfers between devices, passed_along(): return lax.ppermute(block, axis, route)  149 us
    dot_general x32, matrix products, local_part(): jnp.einsum('sbj,bjo->sbo', w.reshape(rows, nleaf, leaf_size), leaf, prefe...  97 us
    ppermute x32, starting transfers between devices, passed_along(): return lax.ppermute(block, axis, route)  63.1 us
    dot_general x32, matrix products, partials_of(): jnp.einsum('sn,crn->csr', w, factors, preferred_element_type=jnp.float32)  52.1 us
    slice x32, local copies, waits for them, and re-layouts, local_part(): right[3].reshape(rank, block_list, block_size)  31.1 us
    slice x32, local copies, waits for them, and re-layouts, local_part(): left[3].reshape(rank, block_list, block_size)  31.1 us
    convert_element_type x32, other arithmetic, advance(): (source.astype(jnp.float32) + incoming.astype(jnp.float32)).astype(jnp.bf...  30 us
  transfers between devices with their start and end apart: 32, of which 32 were waited for; matrix products, arithmetic and copies ran while one was open for 8% of the time, Pallas kernels for 0%

commit v1 on v0

--- a/solution.py
+++ b/solution.py
@@ -80,7 +80,12 @@
         rows = w.shape[0]
         partial_value = partials_of(w, right[:cross])
         sweep_output = local_part(w)
-        gathered = lax.all_gather(partial_value[None], "hodlr", axis=0, tiled=True)
+        gathered = jnp.concatenate(
+            lax.all_to_all(
+                jnp.stack([partial_value[None]] * lax.axis_size("hodlr")), "hodlr", 0, 0
+            ),
+            axis=0,
+        )
         sibling = combine_gathered(gathered, rows)
         return finish(sweep_output, sibling)
 

time: 958 us -> 762 us (0.80)
  blocking collectives: 439 us -> 0 us
  starting transfers between devices: 63.1 us -> 236 us
  waiting for transfers between devices: 149 us -> 193 us
  local copies, waits for them, and re-layouts: 81.8 us -> 107 us
    all_gather x32 -> x0, blocking collectives: 439 us -> none  [apply(): gathered = lax.all_gather(partial_value[None], 'hodlr', axis=0, tiled=True)]
    all_to_all x0 -> x32, starting transfers between devices: none -> 173 us  [apply(): lax.all_to_all(jnp.stack([partial_value[None]] * lax.axis_size('hodlr')),...]
    all_to_all x0 -> x32, waiting for transfers between devices: none -> 77.1 us  [apply(): lax.all_to_all(jnp.stack([partial_value[None]] * lax.axis_size('hodlr')),...]
    ppermute x32, waiting for transfers between devices: 149 us -> 116 us  [passed_along(): return lax.ppermute(block, axis, route)]
    another operation x0 -> x32, local copies, waits for them, and re-layouts: none -> 24.7 us  [apply(): jnp.stack([partial_value[None]] * lax.axis_size('hodlr'))]
  transfers between devices with their start and end apart: 32 -> 64, of which waited for: 32 -> 64; matrix products, arithmetic and copies ran while one was open for 8% -> 24% of each run, Pallas kernels for 0% -> 0%
where the time goes in v1:
time: 762 us; the launch traced here: 753 us
  starting transfers between devices  236 us (31%)
  waiting for transfers between devices  193 us (25%)
  matrix products  183 us (24%)
  local copies, waits for them, and re-layouts  107 us (14%)
  other arithmetic  30.5 us (4%)
    all_to_all x32, starting transfers between devices, apply(): lax.all_to_all(jnp.stack([partial_value[None]] * lax.axis_size('hodlr')),...  173 us
    ppermute x32, waiting for transfers between devices, passed_along(): return lax.ppermute(block, axis, route)  116 us
    dot_general x32, matrix products, local_part(): jnp.einsum('sbj,bjo->sbo', w.reshape(rows, nleaf, leaf_size), leaf, prefe...  96.3 us
    all_to_all x32, waiting for transfers between devices, apply(): lax.all_to_all(jnp.stack([partial_value[None]] * lax.axis_size('hodlr')),...  77.1 us
    ppermute x32, starting transfers between devices, passed_along(): return lax.ppermute(block, axis, route)  63.1 us
    dot_general x32, matrix products, partials_of(): jnp.einsum('sn,crn->csr', w, factors, preferred_element_type=jnp.float32)  52.2 us
    slice x32, local copies, waits for them, and re-layouts, local_part(): left[3].reshape(rank, block_list, block_size)  31.1 us
    slice x32, local copies, waits for them, and re-layouts, local_part(): right[3].reshape(rank, block_list, block_size)  31.1 us
  transfers between devices with their start and end apart: 64, of which 64 were waited for; matrix products, arithmetic and copies ran while one was open for 24% of the time, Pallas kernels for 0%

profile of v1, /device:TPU:7, one launch (start us, length us, event | category | flops | bytes accessed | tf_op | source)
XLA Modules:
  0.0 752.6 jit_solution(3306939226200758390)
XLA Ops:
  0.1 751.9 %while.16 = (s32[]{:T(128)}, bf16[32,2048]{1,0:T(8,128)(2,1)S(1)}, bf16[32,2048]{1,0:T(8,128)(2,1)S(1)}, bf16[32,2048]{1,0:T(8,128)(2,1)}, bf16[2,1024,1024]{2,1...) while((s32[]{:T(128)}, bf16[32,2048]{1,0:T(8,128)(2,1)S(1)}, ...), condition=%wide.region_1.2_spmd.clone, body=%wide.region_0.1_spmd.clone.sunk | while | flops 202575872 | bytes 17322332 | solution.py:110
  6.0 5.1 collective-permute-done
  14.5 5.7 all-to-all-start
  31.2 3.6 collective-permute-done
  38.2 5.4 all-to-all-start
  54.6 3.6 collective-permute-done
  61.6 5.4 all-to-all-start
  78.0 3.6 collective-permute-done
  85.0 5.4 all-to-all-start
  101.3 3.6 collective-permute-done
  108.4 5.4 all-to-all-start
  124.7 3.6 collective-permute-done
  131.8 5.4 all-to-all-start
  148.1 3.6 collective-permute-done
  155.1 5.4 all-to-all-start
  171.5 3.6 collective-permute-done
  178.5 5.4 all-to-all-start
  194.9 3.6 collective-permute-done
  201.9 5.4 all-to-all-start
  218.3 3.6 collective-permute-done
  225.3 5.4 all-to-all-start
  241.7 3.6 collective-permute-done
  248.7 5.4 all-to-all-start
  265.1 3.6 collective-permute-done
  272.1 5.4 all-to-all-start
  288.5 3.6 collective-permute-done
  295.5 5.4 all-to-all-start
  311.8 3.6 collective-permute-done
  318.9 5.4 all-to-all-start
  335.2 3.6 collective-permute-done
  342.3 5.4 all-to-all-start
  358.6 3.6 collective-permute-done
  365.6 5.4 all-to-all-start
  382.0 3.6 collective-permute-done
  389.0 5.4 all-to-all-start
  405.4 3.6 collective-permute-done
  412.4 5.4 all-to-all-start
  428.8 3.6 collective-permute-done
  435.8 5.4 all-to-all-start
  452.2 3.6 collective-permute-done
  459.2 5.4 all-to-all-start
  475.6 3.6 collective-permute-done
  482.6 5.4 all-to-all-start
  499.0 3.6 collective-permute-done
  506.0 5.4 all-to-all-start
  522.4 3.6 collective-permute-done
  529.4 5.4 all-to-all-start
  545.7 3.6 collective-permute-done
  552.8 5.4 all-to-all-start
  569.1 3.6 collective-permute-done
  576.2 5.4 all-to-all-start
  592.5 3.6 collective-permute-done
  599.5 5.4 all-to-all-start
  615.9 3.6 collective-permute-done
  622.9 5.4 all-to-all-start
  639.3 3.6 collective-permute-done
  646.3 5.4 all-to-all-start
  662.7 3.6 collective-permute-done
  669.7 5.4 all-to-all-start
  686.1 3.6 collective-permute-done
  693.1 5.4 all-to-all-start
  716.5 5.4 all-to-all-start
  732.9 3.6 collective-permute-done
  739.9 5.4 all-to-all-start
  (712 shorter events, 463.8 us)
Async XLA Ops:
  0.1 10.9 %collective-permute-start = (bf16[32,2048]{1,0:T(8,128)(2,1)S(1)}, bf16[32,2048]{1,0:T(8,128)(2,1)S(1)}, u32[]{:S(2)}, u32[]{:S(2)}) collective-permute-start(bf16[32,2048]{1,0:T(8,128)(2,1)S(1)} %broadcast_select_fusion.2), channel_id=1, source_target_pairs={{0,8},{8,16},{16,24},{24,32},{32,40},{40,48},{48,56},{56,64},{64,7... | collective-permute-start | bytes 393224 | tf_op jit(solution)/shard_map/while/body/eval_jaxpr/ppermute | solution.py:10
  14.5 11.6 %all-to-all-start = ((f32[8,1,3,2048]{3,1,2,0:T(1,128)}), f32[8,1,3,2048]{3,1,2,0:T(1,128)S(1)}, u32[]{:S(2)}, u32[]{:S(2)}) async-start(f32[8,1,3,2048]{3,1,2,0:T(1,128)} %stack.19), calls=%async_computation | async-start | bytes 393216 | tf_op jit(solution)/shard_map/while/body/eval_jaxpr/all_to_all | solution.py:84
  26.9 7.8 %collective-permute-start = (bf16[32,2048]{1,0:T(8,128)(2,1)S(1)}, bf16[32,2048]{1,0:T(8,128)(2,1)S(1)}, u32[]{:S(2)}, u32[]{:S(2)}) collective-permute-start(bf16[32,2048]{1,0:T(8,128)(2,1)S(1)} %broadcast_select_fusion.2), channel_id=1, source_target_pairs={{0,8},{8,16},{16,24},{24,32},{32,40},{40,48},{48,56},{56,64},{64,7... | collective-permute-start | bytes 393224 | tf_op jit(solution)/shard_map/while/body/eval_jaxpr/ppermute | solution.py:10
  38.2 11.3 %all-to-all-start = ((f32[8,1,3,2048]{3,1,2,0:T(1,128)}), f32[8,1,3,2048]{3,1,2,0:T(1,128)S(1)}, u32[]{:S(2)}, u32[]{:S(2)}) async-start(f32[8,1,3,2048]{3,1,2,0:T(1,128)} %stack.19), calls=%async_computation | async-start | bytes 393216 | tf_op jit(solution)/shard_map/while/body/eval_jaxpr/all_to_all | solution.py:84
  50.3 7.8 %collective-permute-start = (bf16[32,2048]{1,0:T(8,128)(2,1)S(1)}, bf16[32,2048]{1,0:T(8,128)(2,1)S(1)}, u32[]{:S(2)}, u32[]{:S(2)}) collective-permute-start(bf16[32,2048]{1,0:T(8,128)(2,1)S(1)} %broadcast_select_fusion.2), channel_id=1, source_target_pairs={{0,8},{8,16},{16,24},{24,32},{32,40},{40,48},{48,56},{56,64},{64,7... | collective-permute-start | bytes 393224 | tf_op jit(solution)/shard_map/while/body/eval_jaxpr/ppermute | solution.py:10
  61.6 11.3 %all-to-all-start = ((f32[8,1,3,2048]{3,1,2,0:T(1,128)}), f32[8,1,3,2048]{3,1,2,0:T(1,128)S(1)}, u32[]{:S(2)}, u32[]{:S(2)}) async-start(f32[8,1,3,2048]{3,1,2,0:T(1,128)} %stack.19), calls=%async_computation | async-start | bytes 393216 | tf_op jit(solution)/shard_map/while/body/eval_jaxpr/all_to_all | solution.py:84
  73.7 7.8 %collective-permute-start = (bf16[32,2048]{1,0:T(8,128)(2,1)S(1)}, bf16[32,2048]{1,0:T(8,128)(2,1)S(1)}, u32[]{:S(2)}, u32[]{:S(2)}) collective-permute-start(bf16[32,2048]{1,0:T(8,128)(2,1)S(1)} %broadcast_select_fusion.2), channel_id=1, source_target_pairs={{0,8},{8,16},{16,24},{24,32},{32,40},{40,48},{48,56},{56,64},{64,7... | collective-permute-start | bytes 393224 | tf_op jit(solution)/shard_map/while/body/eval_jaxpr/ppermute | solution.py:10
  85.0 11.3 %all-to-all-start = ((f32[8,1,3,2048]{3,1,2,0:T(1,128)}), f32[8,1,3,2048]{3,1,2,0:T(1,128)S(1)}, u32[]{:S(2)}, u32[]{:S(2)}) async-start(f32[8,1,3,2048]{3,1,2,0:T(1,128)} %stack.19), calls=%async_computation | async-start | bytes 393216 | tf_op jit(solution)/shard_map/while/body/eval_jaxpr/all_to_all | solution.py:84
  97.1 7.8 %collective-permute-start = (bf16[32,2048]{1,0:T(8,128)(2,1)S(1)}, bf16[32,2048]{1,0:T(8,128)(2,1)S(1)}, u32[]{:S(2)}, u32[]{:S(2)}) collective-permute-start(bf16[32,2048]{1,0:T(8,128)(2,1)S(1)} %broadcast_select_fusion.2), channel_id=1, source_target_pairs={{0,8},{8,16},{16,24},{24,32},{32,40},{40,48},{48,56},{56,64},{64,7... | collective-permute-start | bytes 393224 | tf_op jit(solution)/shard_map/while/body/eval_jaxpr/ppermute | solution.py:10
  108.4 11.3 %all-to-all-start = ((f32[8,1,3,2048]{3,1,2,0:T(1,128)}), f32[8,1,3,2048]{3,1,2,0:T(1,128)S(1)}, u32[]{:S(2)}, u32[]{:S(2)}) async-start(f32[8,1,3,2048]{3,1,2,0:T(1,128)} %stack.19), calls=%async_computation | async-start | bytes 393216 | tf_op jit(solution)/shard_map/while/body/eval_jaxpr/all_to_all | solution.py:84
  120.5 7.8 %collective-permute-start = (bf16[32,2048]{1,0:T(8,128)(2,1)S(1)}, bf16[32,2048]{1,0:T(8,128)(2,1)S(1)}, u32[]{:S(2)}, u32[]{:S(2)}) collective-permute-start(bf16[32,2048]{1,0:T(8,128)(2,1)S(1)} %broadcast_select_fusion.2), channel_id=1, source_target_pairs={{0,8},{8,16},{16,24},{24,32},{32,40},{40,48},{48,56},{56,64},{64,7... | collective-permute-start | bytes 393224 | tf_op jit(solution)/shard_map/while/body/eval_jaxpr/ppermute | solution.py:10
  131.8 11.3 %all-to-all-start = ((f32[8,1,3,2048]{3,1,2,0:T(1,128)}), f32[8,1,3,2048]{3,1,2,0:T(1,128)S(1)}, u32[]{:S(2)}, u32[]{:S(2)}) async-start(f32[8,1,3,2048]{3,1,2,0:T(1,128)} %stack.19), calls=%async_computation | async-start | bytes 393216 | tf_op jit(solution)/shard_map/while/body/eval_jaxpr/all_to_all | solution.py:84
  143.9 7.8 %collective-permute-start = (bf16[32,2048]{1,0:T(8,128)(2,1)S(1)}, bf16[32,2048]{1,0:T(8,128)(2,1)S(1)}, u32[]{:S(2)}, u32[]{:S(2)}) collective-permute-start(bf16[32,2048]{1,0:T(8,128)(2,1)S(1)} %broadcast_select_fusion.2), channel_id=1, source_target_pairs={{0,8},{8,16},{16,24},{24,32},{32,40},{40,48},{48,56},{56,64},{64,7... | collective-permute-start | bytes 393224 | tf_op jit(solution)/shard_map/while/body/eval_jaxpr/ppermute | solution.py:10
  155.1 11.3 %all-to-all-start = ((f32[8,1,3,2048]{3,1,2,0:T(1,128)}), f32[8,1,3,2048]{3,1,2,0:T(1,128)S(1)}, u32[]{:S(2)}, u32[]{:S(2)}) async-start(f32[8,1,3,2048]{3,1,2,0:T(1,128)} %stack.19), calls=%async_computation | async-start | bytes 393216 | tf_op jit(solution)/shard_map/while/body/eval_jaxpr/all_to_all | solution.py:84
  167.3 7.8 %collective-permute-start = (bf16[32,2048]{1,0:T(8,128)(2,1)S(1)}, bf16[32,2048]{1,0:T(8,128)(2,1)S(1)}, u32[]{:S(2)}, u32[]{:S(2)}) collective-permute-start(bf16[32,2048]{1,0:T(8,128)(2,1)S(1)} %broadcast_select_fusion.2), channel_id=1, source_target_pairs={{0,8},{8,16},{16,24},{24,32},{32,40},{40,48},{48,56},{56,64},{64,7... | collective-permute-start | bytes 393224 | tf_op jit(solution)/shard_map/while/body/eval_jaxpr/ppermute | solution.py:10
  178.5 11.3 %all-to-all-start = ((f32[8,1,3,2048]{3,1,2,0:T(1,128)}), f32[8,1,3,2048]{3,1,2,0:T(1,128)S(1)}, u32[]{:S(2)}, u32[]{:S(2)}) async-start(f32[8,1,3,2048]{3,1,2,0:T(1,128)} %stack.19), calls=%async_computation | async-start | bytes 393216 | tf_op jit(solution)/shard_map/while/body/eval_jaxpr/all_to_all | solution.py:84
  190.6 7.8 %collective-permute-start = (bf16[32,2048]{1,0:T(8,128)(2,1)S(1)}, bf16[32,2048]{1,0:T(8,128)(2,1)S(1)}, u32[]{:S(2)}, u32[]{:S(2)}) collective-permute-start(bf16[32,2048]{1,0:T(8,128)(2,1)S(1)} %broadcast_select_fusion.2), channel_id=1, source_target_pairs={{0,8},{8,16},{16,24},{24,32},{32,40},{40,48},{48,56},{56,64},{64,7... | collective-permute-start | bytes 393224 | tf_op jit(solution)/shard_map/while/body/eval_jaxpr/ppermute | solution.py:10
  201.9 11.3 %all-to-all-start = ((f32[8,1,3,2048]{3,1,2,0:T(1,128)}), f32[8,1,3,2048]{3,1,2,0:T(1,128)S(1)}, u32[]{:S(2)}, u32[]{:S(2)}) async-start(f32[8,1,3,2048]{3,1,2,0:T(1,128)} %stack.19), calls=%async_computation | async-start | bytes 393216 | tf_op jit(solution)/shard_map/while/body/eval_jaxpr/all_to_all | solution.py:84
  214.0 7.8 %collective-permute-start = (bf16[32,2048]{1,0:T(8,128)(2,1)S(1)}, bf16[32,2048]{1,0:T(8,128)(2,1)S(1)}, u32[]{:S(2)}, u32[]{:S(2)}) collective-permute-start(bf16[32,2048]{1,0:T(8,128)(2,1)S(1)} %broadcast_select_fusion.2), channel_id=1, source_target_pairs={{0,8},{8,16},{16,24},{24,32},{32,40},{40,48},{48,56},{56,64},{64,7... | collective-permute-start | bytes 393224 | tf_op jit(solution)/shard_map/while/body/eval_jaxpr/ppermute | solution.py:10
  225.3 11.3 %all-to-all-start = ((f32[8,1,3,2048]{3,1,2,0:T(1,128)}), f32[8,1,3,2048]{3,1,2,0:T(1,128)S(1)}, u32[]{:S(2)}, u32[]{:S(2)}) async-start(f32[8,1,3,2048]{3,1,2,0:T(1,128)} %stack.19), calls=%async_computation | async-start | bytes 393216 | tf_op jit(solution)/shard_map/while/body/eval_jaxpr/all_to_all | solution.py:84
  237.4 7.8 %collective-permute-start = (bf16[32,2048]{1,0:T(8,128)(2,1)S(1)}, bf16[32,2048]{1,0:T(8,128)(2,1)S(1)}, u32[]{:S(2)}, u32[]{:S(2)}) collective-permute-start(bf16[32,2048]{1,0:T(8,128)(2,1)S(1)} %broadcast_select_fusion.2), channel_id=1, source_target_pairs={{0,8},{8,16},{16,24},{24,32},{32,40},{40,48},{48,56},{56,64},{64,7... | collective-permute-start | bytes 393224 | tf_op jit(solution)/shard_map/while/body/eval_jaxpr/ppermute | solution.py:10
  248.7 11.3 %all-to-all-start = ((f32[8,1,3,2048]{3,1,2,0:T(1,128)}), f32[8,1,3,2048]{3,1,2,0:T(1,128)S(1)}, u32[]{:S(2)}, u32[]{:S(2)}) async-start(f32[8,1,3,2048]{3,1,2,0:T(1,128)} %stack.19), calls=%async_computation | async-start | bytes 393216 | tf_op jit(solution)/shard_map/while/body/eval_jaxpr/all_to_all | solution.py:84
  260.8 7.8 %collective-permute-start = (bf16[32,2048]{1,0:T(8,128)(2,1)S(1)}, bf16[32,2048]{1,0:T(8,128)(2,1)S(1)}, u32[]{:S(2)}, u32[]{:S(2)}) collective-permute-start(bf16[32,2048]{1,0:T(8,128)(2,1)S(1)} %broadcast_select_fusion.2), channel_id=1, source_target_pairs={{0,8},{8,16},{16,24},{24,32},{32,40},{40,48},{48,56},{56,64},{64,7... | collective-permute-start | bytes 393224 | tf_op jit(solution)/shard_map/while/body/eval_jaxpr/ppermute | solution.py:10
  272.1 11.3 %all-to-all-start = ((f32[8,1,3,2048]{3,1,2,0:T(1,128)}), f32[8,1,3,2048]{3,1,2,0:T(1,128)S(1)}, u32[]{:S(2)}, u32[]{:S(2)}) async-start(f32[8,1,3,2048]{3,1,2,0:T(1,128)} %stack.19), calls=%async_computation | async-start | bytes 393216 | tf_op jit(solution)/shard_map/while/body/eval_jaxpr/all_to_all | solution.py:84
  284.2 7.8 %collective-permute-start = (bf16[32,2048]{1,0:T(8,128)(2,1)S(1)}, bf16[32,2048]{1,0:T(8,128)(2,1)S(1)}, u32[]{:S(2)}, u32[]{:S(2)}) collective-permute-start(bf16[32,2048]{1,0:T(8,128)(2,1)S(1)} %broadcast_select_fusion.2), channel_id=1, source_target_pairs={{0,8},{8,16},{16,24},{24,32},{32,40},{40,48},{48,56},{56,64},{64,7... | collective-permute-start | bytes 393224 | tf_op jit(solution)/shard_map/while/body/eval_jaxpr/ppermute | solution.py:10
  295.5 11.3 %all-to-all-start = ((f32[8,1,3,2048]{3,1,2,0:T(1,128)}), f32[8,1,3,2048]{3,1,2,0:T(1,128)S(1)}, u32[]{:S(2)}, u32[]{:S(2)}) async-start(f32[8,1,3,2048]{3,1,2,0:T(1,128)} %stack.19), calls=%async_computation | async-start | bytes 393216 | tf_op jit(solution)/shard_map/while/body/eval_jaxpr/all_to_all | solution.py:84
  307.6 7.8 %collective-permute-start = (bf16[32,2048]{1,0:T(8,128)(2,1)S(1)}, bf16[32,2048]{1,0:T(8,128)(2,1)S(1)}, u32[]{:S(2)}, u32[]{:S(2)}) collective-permute-start(bf16[32,2048]{1,0:T(8,128)(2,1)S(1)} %broadcast_select_fusion.2), channel_id=1, source_target_pairs={{0,8},{8,16},{16,24},{24,32},{32,40},{40,48},{48,56},{56,64},{64,7... | collective-permute-start | bytes 393224 | tf_op jit(solution)/shard_map/while/body/eval_jaxpr/ppermute | solution.py:10
  318.9 11.3 %all-to-all-start = ((f32[8,1,3,2048]{3,1,2,0:T(1,128)}), f32[8,1,3,2048]{3,1,2,0:T(1,128)S(1)}, u32[]{:S(2)}, u32[]{:S(2)}) async-start(f32[8,1,3,2048]{3,1,2,0:T(1,128)} %stack.19), calls=%async_computation | async-start | bytes 393216 | tf_op jit(solution)/shard_map/while/body/eval_jaxpr/all_to_all | solution.py:84
  331.0 7.8 %collective-permute-start = (bf16[32,2048]{1,0:T(8,128)(2,1)S(1)}, bf16[32,2048]{1,0:T(8,128)(2,1)S(1)}, u32[]{:S(2)}, u32[]{:S(2)}) collective-permute-start(bf16[32,2048]{1,0:T(8,128)(2,1)S(1)} %broadcast_select_fusion.2), channel_id=1, source_target_pairs={{0,8},{8,16},{16,24},{24,32},{32,40},{40,48},{48,56},{56,64},{64,7... | collective-permute-start | bytes 393224 | tf_op jit(solution)/shard_map/while/body/eval_jaxpr/ppermute | solution.py:10
  342.3 11.3 %all-to-all-start = ((f32[8,1,3,2048]{3,1,2,0:T(1,128)}), f32[8,1,3,2048]{3,1,2,0:T(1,128)S(1)}, u32[]{:S(2)}, u32[]{:S(2)}) async-start(f32[8,1,3,2048]{3,1,2,0:T(1,128)} %stack.19), calls=%async_computation | async-start | bytes 393216 | tf_op jit(solution)/shard_map/while/body/eval_jaxpr/all_to_all | solution.py:84
  354.4 7.8 %collective-permute-start = (bf16[32,2048]{1,0:T(8,128)(2,1)S(1)}, bf16[32,2048]{1,0:T(8,128)(2,1)S(1)}, u32[]{:S(2)}, u32[]{:S(2)}) collective-permute-start(bf16[32,2048]{1,0:T(8,128)(2,1)S(1)} %broadcast_select_fusion.2), channel_id=1, source_target_pairs={{0,8},{8,16},{16,24},{24,32},{32,40},{40,48},{48,56},{56,64},{64,7... | collective-permute-start | bytes 393224 | tf_op jit(solution)/shard_map/while/body/eval_jaxpr/ppermute | solution.py:10
  365.6 11.3 %all-to-all-start = ((f32[8,1,3,2048]{3,1,2,0:T(1,128)}), f32[8,1,3,2048]{3,1,2,0:T(1,128)S(1)}, u32[]{:S(2)}, u32[]{:S(2)}) async-start(f32[8,1,3,2048]{3,1,2,0:T(1,128)} %stack.19), calls=%async_computation | async-start | bytes 393216 | tf_op jit(solution)/shard_map/while/body/eval_jaxpr/all_to_all | solution.py:84
  377.8 7.8 %collective-permute-start = (bf16[32,2048]{1,0:T(8,128)(2,1)S(1)}, bf16[32,2048]{1,0:T(8,128)(2,1)S(1)}, u32[]{:S(2)}, u32[]{:S(2)}) collective-permute-start(bf16[32,2048]{1,0:T(8,128)(2,1)S(1)} %broadcast_select_fusion.2), channel_id=1, source_target_pairs={{0,8},{8,16},{16,24},{24,32},{32,40},{40,48},{48,56},{56,64},{64,7... | collective-permute-start | bytes 393224 | tf_op jit(solution)/shard_map/while/body/eval_jaxpr/ppermute | solution.py:10
  389.0 11.3 %all-to-all-start = ((f32[8,1,3,2048]{3,1,2,0:T(1,128)}), f32[8,1,3,2048]{3,1,2,0:T(1,128)S(1)}, u32[]{:S(2)}, u32[]{:S(2)}) async-start(f32[8,1,3,2048]{3,1,2,0:T(1,128)} %stack.19), calls=%async_computation | async-start | bytes 393216 | tf_op jit(solution)/shard_map/while/body/eval_jaxpr/all_to_all | solution.py:84
  401.1 7.8 %collective-permute-start = (bf16[32,2048]{1,0:T(8,128)(2,1)S(1)}, bf16[32,2048]{1,0:T(8,128)(2,1)S(1)}, u32[]{:S(2)}, u32[]{:S(2)}) collective-permute-start(bf16[32,2048]{1,0:T(8,128)(2,1)S(1)} %broadcast_select_fusion.2), channel_id=1, source_target_pairs={{0,8},{8,16},{16,24},{24,32},{32,40},{40,48},{48,56},{56,64},{64,7... | collective-permute-start | bytes 393224 | tf_op jit(solution)/shard_map/while/body/eval_jaxpr/ppermute | solution.py:10
  412.4 11.3 %all-to-all-start = ((f32[8,1,3,2048]{3,1,2,0:T(1,128)}), f32[8,1,3,2048]{3,1,2,0:T(1,128)S(1)}, u32[]{:S(2)}, u32[]{:S(2)}) async-start(f32[8,1,3,2048]{3,1,2,0:T(1,128)} %stack.19), calls=%async_computation | async-start | bytes 393216 | tf_op jit(solution)/shard_map/while/body/eval_jaxpr/all_to_all | solution.py:84
  424.5 7.8 %collective-permute-start = (bf16[32,2048]{1,0:T(8,128)(2,1)S(1)}, bf16[32,2048]{1,0:T(8,128)(2,1)S(1)}, u32[]{:S(2)}, u32[]{:S(2)}) collective-permute-start(bf16[32,2048]{1,0:T(8,128)(2,1)S(1)} %broadcast_select_fusion.2), channel_id=1, source_target_pairs={{0,8},{8,16},{16,24},{24,32},{32,40},{40,48},{48,56},{56,64},{64,7... | collective-permute-start | bytes 393224 | tf_op jit(solution)/shard_map/while/body/eval_jaxpr/ppermute | solution.py:10
  435.8 11.3 %all-to-all-start = ((f32[8,1,3,2048]{3,1,2,0:T(1,128)}), f32[8,1,3,2048]{3,1,2,0:T(1,128)S(1)}, u32[]{:S(2)}, u32[]{:S(2)}) async-start(f32[8,1,3,2048]{3,1,2,0:T(1,128)} %stack.19), calls=%async_computation | async-start | bytes 393216 | tf_op jit(solution)/shard_map/while/body/eval_jaxpr/all_to_all | solution.py:84
  447.9 7.8 %collective-permute-start = (bf16[32,2048]{1,0:T(8,128)(2,1)S(1)}, bf16[32,2048]{1,0:T(8,128)(2,1)S(1)}, u32[]{:S(2)}, u32[]{:S(2)}) collective-permute-start(bf16[32,2048]{1,0:T(8,128)(2,1)S(1)} %broadcast_select_fusion.2), channel_id=1, source_target_pairs={{0,8},{8,16},{16,24},{24,32},{32,40},{40,48},{48,56},{56,64},{64,7... | collective-permute-start | bytes 393224 | tf_op jit(solution)/shard_map/while/body/eval_jaxpr/ppermute | solution.py:10
  459.2 11.3 %all-to-all-start = ((f32[8,1,3,2048]{3,1,2,0:T(1,128)}), f32[8,1,3,2048]{3,1,2,0:T(1,128)S(1)}, u32[]{:S(2)}, u32[]{:S(2)}) async-start(f32[8,1,3,2048]{3,1,2,0:T(1,128)} %stack.19), calls=%async_computation | async-start | bytes 393216 | tf_op jit(solution)/shard_map/while/body/eval_jaxpr/all_to_all | solution.py:84
  471.3 7.8 %collective-permute-start = (bf16[32,2048]{1,0:T(8,128)(2,1)S(1)}, bf16[32,2048]{1,0:T(8,128)(2,1)S(1)}, u32[]{:S(2)}, u32[]{:S(2)}) collective-permute-start(bf16[32,2048]{1,0:T(8,128)(2,1)S(1)} %broadcast_select_fusion.2), channel_id=1, source_target_pairs={{0,8},{8,16},{16,24},{24,32},{32,40},{40,48},{48,56},{56,64},{64,7... | collective-permute-start | bytes 393224 | tf_op jit(solution)/shard_map/while/body/eval_jaxpr/ppermute | solution.py:10
  482.6 11.3 %all-to-all-start = ((f32[8,1,3,2048]{3,1,2,0:T(1,128)}), f32[8,1,3,2048]{3,1,2,0:T(1,128)S(1)}, u32[]{:S(2)}, u32[]{:S(2)}) async-start(f32[8,1,3,2048]{3,1,2,0:T(1,128)} %stack.19), calls=%async_computation | async-start | bytes 393216 | tf_op jit(solution)/shard_map/while/body/eval_jaxpr/all_to_all | solution.py:84
  494.7 7.8 %collective-permute-start = (bf16[32,2048]{1,0:T(8,128)(2,1)S(1)}, bf16[32,2048]{1,0:T(8,128)(2,1)S(1)}, u32[]{:S(2)}, u32[]{:S(2)}) collective-permute-start(bf16[32,2048]{1,0:T(8,128)(2,1)S(1)} %broadcast_select_fusion.2), channel_id=1, source_target_pairs={{0,8},{8,16},{16,24},{24,32},{32,40},{40,48},{48,56},{56,64},{64,7... | collective-permute-start | bytes 393224 | tf_op jit(solution)/shard_map/while/body/eval_jaxpr/ppermute | solution.py:10
  506.0 11.3 %all-to-all-start = ((f32[8,1,3,2048]{3,1,2,0:T(1,128)}), f32[8,1,3,2048]{3,1,2,0:T(1,128)S(1)}, u32[]{:S(2)}, u32[]{:S(2)}) async-start(f32[8,1,3,2048]{3,1,2,0:T(1,128)} %stack.19), calls=%async_computation | async-start | bytes 393216 | tf_op jit(solution)/shard_map/while/body/eval_jaxpr/all_to_all | solution.py:84
  518.1 7.8 %collective-permute-start = (bf16[32,2048]{1,0:T(8,128)(2,1)S(1)}, bf16[32,2048]{1,0:T(8,128)(2,1)S(1)}, u32[]{:S(2)}, u32[]{:S(2)}) collective-permute-start(bf16[32,2048]{1,0:T(8,128)(2,1)S(1)} %broadcast_select_fusion.2), channel_id=1, source_target_pairs={{0,8},{8,16},{16,24},{24,32},{32,40},{40,48},{48,56},{56,64},{64,7... | collective-permute-start | bytes 393224 | tf_op jit(solution)/shard_map/while/body/eval_jaxpr/ppermute | solution.py:10
  529.4 11.3 %all-to-all-start = ((f32[8,1,3,2048]{3,1,2,0:T(1,128)}), f32[8,1,3,2048]{3,1,2,0:T(1,128)S(1)}, u32[]{:S(2)}, u32[]{:S(2)}) async-start(f32[8,1,3,2048]{3,1,2,0:T(1,128)} %stack.19), calls=%async_computation | async-start | bytes 393216 | tf_op jit(solution)/shard_map/while/body/eval_jaxpr/all_to_all | solution.py:84
  541.5 7.8 %collective-permute-start = (bf16[32,2048]{1,0:T(8,128)(2,1)S(1)}, bf16[32,2048]{1,0:T(8,128)(2,1)S(1)}, u32[]{:S(2)}, u32[]{:S(2)}) collective-permute-start(bf16[32,2048]{1,0:T(8,128)(2,1)S(1)} %broadcast_select_fusion.2), channel_id=1, source_target_pairs={{0,8},{8,16},{16,24},{24,32},{32,40},{40,48},{48,56},{56,64},{64,7... | collective-permute-start | bytes 393224 | tf_op jit(solution)/shard_map/while/body/eval_jaxpr/ppermute | solution.py:10
  552.8 11.3 %all-to-all-start = ((f32[8,1,3,2048]{3,1,2,0:T(1,128)}), f32[8,1,3,2048]{3,1,2,0:T(1,128)S(1)}, u32[]{:S(2)}, u32[]{:S(2)}) async-start(f32[8,1,3,2048]{3,1,2,0:T(1,128)} %stack.19), calls=%async_computation | async-start | bytes 393216 | tf_op jit(solution)/shard_map/while/body/eval_jaxpr/all_to_all | solution.py:84
  564.9 7.8 %collective-permute-start = (bf16[32,2048]{1,0:T(8,128)(2,1)S(1)}, bf16[32,2048]{1,0:T(8,128)(2,1)S(1)}, u32[]{:S(2)}, u32[]{:S(2)}) collective-permute-start(bf16[32,2048]{1,0:T(8,128)(2,1)S(1)} %broadcast_select_fusion.2), channel_id=1, source_target_pairs={{0,8},{8,16},{16,24},{24,32},{32,40},{40,48},{48,56},{56,64},{64,7... | collective-permute-start | bytes 393224 | tf_op jit(solution)/shard_map/while/body/eval_jaxpr/ppermute | solution.py:10
  576.2 11.3 %all-to-all-start = ((f32[8,1,3,2048]{3,1,2,0:T(1,128)}), f32[8,1,3,2048]{3,1,2,0:T(1,128)S(1)}, u32[]{:S(2)}, u32[]{:S(2)}) async-start(f32[8,1,3,2048]{3,1,2,0:T(1,128)} %stack.19), calls=%async_computation | async-start | bytes 393216 | tf_op jit(solution)/shard_map/while/body/eval_jaxpr/all_to_all | solution.py:84
  588.3 7.8 %collective-permute-start = (bf16[32,2048]{1,0:T(8,128)(2,1)S(1)}, bf16[32,2048]{1,0:T(8,128)(2,1)S(1)}, u32[]{:S(2)}, u32[]{:S(2)}) collective-permute-start(bf16[32,2048]{1,0:T(8,128)(2,1)S(1)} %broadcast_select_fusion.2), channel_id=1, source_target_pairs={{0,8},{8,16},{16,24},{24,32},{32,40},{40,48},{48,56},{56,64},{64,7... | collective-permute-start | bytes 393224 | tf_op jit(solution)/shard_map/while/body/eval_jaxpr/ppermute | solution.py:10
  599.5 11.3 %all-to-all-start = ((f32[8,1,3,2048]{3,1,2,0:T(1,128)}), f32[8,1,3,2048]{3,1,2,0:T(1,128)S(1)}, u32[]{:S(2)}, u32[]{:S(2)}) async-start(f32[8,1,3,2048]{3,1,2,0:T(1,128)} %stack.19), calls=%async_computation | async-start | bytes 393216 | tf_op jit(solution)/shard_map/while/body/eval_jaxpr/all_to_all | solution.py:84
  611.7 7.8 %collective-permute-start = (bf16[32,2048]{1,0:T(8,128)(2,1)S(1)}, bf16[32,2048]{1,0:T(8,128)(2,1)S(1)}, u32[]{:S(2)}, u32[]{:S(2)}) collective-permute-start(bf16[32,2048]{1,0:T(8,128)(2,1)S(1)} %broadcast_select_fusion.2), channel_id=1, source_target_pairs={{0,8},{8,16},{16,24},{24,32},{32,40},{40,48},{48,56},{56,64},{64,7... | collective-permute-start | bytes 393224 | tf_op jit(solution)/shard_map/while/body/eval_jaxpr/ppermute | solution.py:10
  622.9 11.3 %all-to-all-start = ((f32[8,1,3,2048]{3,1,2,0:T(1,128)}), f32[8,1,3,2048]{3,1,2,0:T(1,128)S(1)}, u32[]{:S(2)}, u32[]{:S(2)}) async-start(f32[8,1,3,2048]{3,1,2,0:T(1,128)} %stack.19), calls=%async_computation | async-start | bytes 393216 | tf_op jit(solution)/shard_map/while/body/eval_jaxpr/all_to_all | solution.py:84
  635.0 7.8 %collective-permute-start = (bf16[32,2048]{1,0:T(8,128)(2,1)S(1)}, bf16[32,2048]{1,0:T(8,128)(2,1)S(1)}, u32[]{:S(2)}, u32[]{:S(2)}) collective-permute-start(bf16[32,2048]{1,0:T(8,128)(2,1)S(1)} %broadcast_select_fusion.2), channel_id=1, source_target_pairs={{0,8},{8,16},{16,24},{24,32},{32,40},{40,48},{48,56},{56,64},{64,7... | collective-permute-start | bytes 393224 | tf_op jit(solution)/shard_map/while/body/eval_jaxpr/ppermute | solution.py:10
  646.3 11.3 %all-to-all-start = ((f32[8,1,3,2048]{3,1,2,0:T(1,128)}), f32[8,1,3,2048]{3,1,2,0:T(1,128)S(1)}, u32[]{:S(2)}, u32[]{:S(2)}) async-start(f32[8,1,3,2048]{3,1,2,0:T(1,128)} %stack.19), calls=%async_computation | async-start | bytes 393216 | tf_op jit(solution)/shard_map/while/body/eval_jaxpr/all_to_all | solution.py:84
  658.4 7.8 %collective-permute-start = (bf16[32,2048]{1,0:T(8,128)(2,1)S(1)}, bf16[32,2048]{1,0:T(8,128)(2,1)S(1)}, u32[]{:S(2)}, u32[]{:S(2)}) collective-permute-start(bf16[32,2048]{1,0:T(8,128)(2,1)S(1)} %broadcast_select_fusion.2), channel_id=1, source_target_pairs={{0,8},{8,16},{16,24},{24,32},{32,40},{40,48},{48,56},{56,64},{64,7... | collective-permute-start | bytes 393224 | tf_op jit(solution)/shard_map/while/body/eval_jaxpr/ppermute | solution.py:10
  669.7 11.3 %all-to-all-start = ((f32[8,1,3,2048]{3,1,2,0:T(1,128)}), f32[8,1,3,2048]{3,1,2,0:T(1,128)S(1)}, u32[]{:S(2)}, u32[]{:S(2)}) async-start(f32[8,1,3,2048]{3,1,2,0:T(1,128)} %stack.19), calls=%async_computation | async-start | bytes 393216 | tf_op jit(solution)/shard_map/while/body/eval_jaxpr/all_to_all | solution.py:84
  681.8 7.8 %collective-permute-start = (bf16[32,2048]{1,0:T(8,128)(2,1)S(1)}, bf16[32,2048]{1,0:T(8,128)(2,1)S(1)}, u32[]{:S(2)}, u32[]{:S(2)}) collective-permute-start(bf16[32,2048]{1,0:T(8,128)(2,1)S(1)} %broadcast_select_fusion.2), channel_id=1, source_target_pairs={{0,8},{8,16},{16,24},{24,32},{32,40},{40,48},{48,56},{56,64},{64,7... | collective-permute-start | bytes 393224 | tf_op jit(solution)/shard_map/while/body/eval_jaxpr/ppermute | solution.py:10
  693.1 11.3 %all-to-all-start = ((f32[8,1,3,2048]{3,1,2,0:T(1,128)}), f32[8,1,3,2048]{3,1,2,0:T(1,128)S(1)}, u32[]{:S(2)}, u32[]{:S(2)}) async-start(f32[8,1,3,2048]{3,1,2,0:T(1,128)} %stack.19), calls=%async_computation | async-start | bytes 393216 | tf_op jit(solution)/shard_map/while/body/eval_jaxpr/all_to_all | solution.py:84
  705.2 7.8 %collective-permute-start = (bf16[32,2048]{1,0:T(8,128)(2,1)S(1)}, bf16[32,2048]{1,0:T(8,128)(2,1)S(1)}, u32[]{:S(2)}, u32[]{:S(2)}) collective-permute-start(bf16[32,2048]{1,0:T(8,128)(2,1)S(1)} %broadcast_select_fusion.2), channel_id=1, source_target_pairs={{0,8},{8,16},{16,24},{24,32},{32,40},{40,48},{48,56},{56,64},{64,7... | collective-permute-start | bytes 393224 | tf_op jit(solution)/shard_map/while/body/eval_jaxpr/ppermute | solution.py:10
  716.5 11.3 %all-to-all-start = ((f32[8,1,3,2048]{3,1,2,0:T(1,128)}), f32[8,1,3,2048]{3,1,2,0:T(1,128)S(1)}, u32[]{:S(2)}, u32[]{:S(2)}) async-start(f32[8,1,3,2048]{3,1,2,0:T(1,128)} %stack.19), calls=%async_computation | async-start | bytes 393216 | tf_op jit(solution)/shard_map/while/body/eval_jaxpr/all_to_all | solution.py:84
  728.6 7.8 %collective-permute-start = (bf16[32,2048]{1,0:T(8,128)(2,1)S(1)}, bf16[32,2048]{1,0:T(8,128)(2,1)S(1)}, u32[]{:S(2)}, u32[]{:S(2)}) collective-permute-start(bf16[32,2048]{1,0:T(8,128)(2,1)S(1)} %broadcast_select_fusion.2), channel_id=1, source_target_pairs={{0,8},{8,16},{16,24},{24,32},{32,40},{40,48},{48,56},{56,64},{64,7... | collective-permute-start | bytes 393224 | tf_op jit(solution)/shard_map/while/body/eval_jaxpr/ppermute | solution.py:10
  739.9 11.3 %all-to-all-start = ((f32[8,1,3,2048]{3,1,2,0:T(1,128)}), f32[8,1,3,2048]{3,1,2,0:T(1,128)S(1)}, u32[]{:S(2)}, u32[]{:S(2)}) async-start(f32[8,1,3,2048]{3,1,2,0:T(1,128)} %stack.19), calls=%async_computation | async-start | bytes 393216 | tf_op jit(solution)/shard_map/while/body/eval_jaxpr/all_to_all | solution.py:84
  (33 other events, 457.7 us)
